TPU v7x, 512 devices: a whole 4x4x16 slice. The times are simulated.
512 devices in a mesh: doc: 16 (over y_hi, x, core), seq: 32 (over z, y_lo).
Axes of the slice: x: 4, y: 4 (y_hi: 2, y_lo: 2; y = y_hi * 2 + y_lo), z: 16, core: 2. Of those that a mesh axis runs over, the one named last changes fastest.
Arguments:
- queries: bfloat16 [16, 4096, 1024], P('doc', 'seq'), may hold values from -7 to 7
- key_rows: bfloat16 [16, 4096, 1024], P('doc', 'seq'), may hold values from -7 to 7
- value_rows: bfloat16 [16, 4096, 1024], P('doc', 'seq'), may hold values from -5 to 5
- cotangent: bfloat16 [16, 4096, 1024], P('doc', 'seq'), may hold values from -3 to 3
- out_weight: bfloat16 [1024, 1024], P('doc'), may hold values from -0.1875 to 0.1875
- lengths: int32 [16, 4], P('doc'), may hold values from 1 to 32, 64 in all within a row
- upweight: int32 [16, 4], P('doc'), may hold values from 1 to 6, as said below
Outputs:
- layer_out: bfloat16 [16, 4096, 1024], P('doc', 'seq')
- grad_query: bfloat16 [16, 4096, 1024], P('doc', 'seq')
- grad_key: bfloat16 [16, 4096, 1024], P('doc', 'seq')
- grad_value: bfloat16 [16, 4096, 1024], P('doc', 'seq')
- grad_weight: float32 [1024, 1024], P('doc')
Inputs may be any that keep to these rules, and one draw needn't show every extreme that they name: Each sequence's documents fill it exactly: the lengths add up to 64, and the longest is 32. `upweight`: each entry is 1 or 6; every sequence has a document with factor 6.
All inputs are finite; a program needn't handle non-finite values.
Results may differ from a plain program's by a relative error of at most 0.0089.
Values may be sent and summed in bfloat16 or wider, within the bound.
A program may use at most 128 MiB of HBM per device.

v0:
```python
import math
import jax
import jax.numpy as jnp
from jax import lax
from jax.sharding import PartitionSpec as P

HEADS = 16
HEAD_DIM = 64
WINDOW = 512
BLOCK = 64
DOCS = 4


def shifted(value, axis, steps):
    count = lax.axis_size(axis)
    first, last = (max(0, -steps), min(count, count - steps))
    return lax.ppermute(value, axis, [(source, source + steps) for source in range(first, last)])


def document_ids(lengths_row, positions):
    bounds = jnp.cumsum(lengths_row) * BLOCK
    return jnp.sum((positions[:, None] >= bounds[None, :]).astype(jnp.int32), axis=1)


def band_mask(query_pos, key_pos, query_doc, key_doc, seq_len):
    near_band = jnp.abs(query_pos[:, None] - key_pos[None, :]) <= WINDOW
    inside = (key_pos >= 0) & (key_pos < seq_len)
    return near_band & inside[None, :] & (query_doc[:, None] == key_doc[None, :])


def soft_weights(query_grp, key_grp, allowed):
    scores = jnp.einsum(
        "qhd,khd->hqk", query_grp, key_grp, preferred_element_type=jnp.float32
    ) * HEAD_DIM ** (-0.5)
    scores = jnp.where(allowed[None], scores, -jnp.inf)
    row_peak = jnp.max(scores, axis=2, keepdims=True)
    exponent = jnp.exp(scores - row_peak)
    return exponent / jnp.sum(exponent, axis=2, keepdims=True)


def body(queries, key_rows, value_rows, cotangent, out_weight, lengths, upweight):
    rows_here = queries.shape[1]
    model_width = queries.shape[2]
    seq_count = lax.axis_size("seq")
    doc_count = lax.axis_size("doc")
    seq_place = lax.axis_index("seq")
    seq_len = rows_here * seq_count
    edge_rows = min(WINDOW, rows_here)
    far_blocks = WINDOW // edge_rows
    key_span = rows_here + 2 * WINDOW
    score_scale = HEAD_DIM ** (-0.5)
    query_rows = queries[0]
    stacked = jnp.stack([key_rows[0], value_rows[0]])
    before_list = [shifted(stacked, "seq", distance) for distance in range(1, far_blocks + 1)]
    after_list = [shifted(stacked, "seq", -distance) for distance in range(1, far_blocks + 1)]
    extended = jnp.concatenate(before_list[::-1] + [stacked] + after_list, axis=1)
    key_ext = extended[0]
    value_ext = extended[1]
    row_base = seq_place * rows_here
    query_pos = row_base + jnp.arange(rows_here, dtype=jnp.int32)
    key_pos = row_base - WINDOW + jnp.arange(key_span, dtype=jnp.int32)
    lengths_row = lengths[0]
    query_doc = document_ids(lengths_row, query_pos)
    allowed = band_mask(query_pos, key_pos, query_doc, document_ids(lengths_row, key_pos), seq_len)
    matches = query_doc[:, None] == jnp.arange(DOCS, dtype=jnp.int32)[None, :]
    token_weight = jnp.sum(jnp.where(matches, upweight[0][None, :], 0), axis=1).astype(jnp.float32)
    group_heads = min(HEADS, max(1, 512 // rows_here))
    group_count = HEADS // group_heads
    group_cols = group_heads * HEAD_DIM

    def group_slices(group_index):
        col_start = group_index * group_cols
        query_grp = lax.dynamic_slice_in_dim(query_rows, col_start, group_cols, 1).reshape(
            rows_here, group_heads, HEAD_DIM
        )
        key_grp = lax.dynamic_slice_in_dim(key_ext, col_start, group_cols, 1).reshape(
            key_span, group_heads, HEAD_DIM
        )
        value_grp = lax.dynamic_slice_in_dim(value_ext, col_start, group_cols, 1).reshape(
            key_span, group_heads, HEAD_DIM
        )
        return (col_start, query_grp, key_grp, value_grp)

    def forward_group(group_index, attended_buf):
        col_start, query_grp, key_grp, value_grp = group_slices(group_index)
        prob_half = soft_weights(query_grp, key_grp, allowed).astype(jnp.bfloat16)
        mixed_rows = jnp.einsum(
            "hqk,khd->qhd", prob_half, value_grp, preferred_element_type=jnp.float32
        )
        mixed_rows = mixed_rows.reshape(rows_here, group_cols).astype(jnp.bfloat16)
        return lax.dynamic_update_slice_in_dim(attended_buf, mixed_rows, col_start, 1)

    attended = lax.fori_loop(
        0, group_count, forward_group, jnp.zeros((rows_here, model_width), jnp.bfloat16)
    )
    full_weight = lax.all_gather(out_weight, "doc", axis=0, tiled=True)
    layer_out = jnp.dot(attended, full_weight, preferred_element_type=jnp.float32).astype(
        jnp.bfloat16
    )
    grad_out = (token_weight[:, None] * cotangent[0].astype(jnp.float32)).astype(jnp.bfloat16)
    grad_attended = lax.dot_general(
        grad_out, full_weight, (((1,), (1,)), ((), ())), preferred_element_type=jnp.float32
    ).astype(jnp.bfloat16)
    partial_grad = lax.dot_general(
        attended, grad_out, (((0,), (0,)), ((), ())), preferred_element_type=jnp.float32
    )
    row_block = lax.psum_scatter(partial_grad, "doc", scatter_dimension=0, tiled=True)
    weight_sum = lax.psum(row_block, "seq")
    grad_weight = weight_sum * (1.0 / math.sqrt(rows_here * seq_count * doc_count))

    def backward_group(group_index, grad_state):
        grad_query_buf, own_grad, early_grad, later_grad = grad_state
        col_start, query_grp, key_grp, value_grp = group_slices(group_index)
        prob_full = soft_weights(query_grp, key_grp, allowed)
        prob_half = prob_full.astype(jnp.bfloat16)
        grad_grp = lax.dynamic_slice_in_dim(grad_attended, col_start, group_cols, 1).reshape(
            rows_here, group_heads, HEAD_DIM
        )
        grad_prob = jnp.einsum(
            "qhd,khd->hqk", grad_grp, value_grp, preferred_element_type=jnp.float32
        )
        centre = jnp.sum(prob_full * grad_prob, axis=2, keepdims=True)
        grad_score = (prob_full * (grad_prob - centre) * score_scale).astype(jnp.bfloat16)
        grad_query_grp = jnp.einsum(
            "hqk,khd->qhd", grad_score, key_grp, preferred_element_type=jnp.float32
        )
        grad_query_grp = grad_query_grp.reshape(rows_here, group_cols).astype(jnp.bfloat16)
        key_part = jnp.einsum(
            "hqk,qhd->khd", grad_score, query_grp, preferred_element_type=jnp.float32
        )
        value_part = jnp.einsum(
            "hqk,qhd->khd", prob_half, grad_grp, preferred_element_type=jnp.float32
        )
        both_parts = jnp.stack(
            [key_part.reshape(key_span, group_cols), value_part.reshape(key_span, group_cols)]
        )
        grad_query_buf = lax.dynamic_update_slice_in_dim(
            grad_query_buf, grad_query_grp, col_start, 1
        )
        own_grad = lax.dynamic_update_slice(
            own_grad, both_parts[:, WINDOW : WINDOW + rows_here], (0, 0, col_start)
        )
        early_grad = lax.dynamic_update_slice(
            early_grad, both_parts[:, :WINDOW].astype(jnp.bfloat16), (0, 0, col_start)
        )
        later_grad = lax.dynamic_update_slice(
            later_grad, both_parts[:, WINDOW + rows_here :].astype(jnp.bfloat16), (0, 0, col_start)
        )
        return (grad_query_buf, own_grad, early_grad, later_grad)

    grad_state = (
        jnp.zeros((rows_here, model_width), jnp.bfloat16),
        jnp.zeros((2, rows_here, model_width), jnp.float32),
        jnp.zeros((2, WINDOW, model_width), jnp.bfloat16),
        jnp.zeros((2, WINDOW, model_width), jnp.bfloat16),
    )
    grad_query, own_grad, early_grad, later_grad = lax.fori_loop(
        0, group_count, backward_group, grad_state
    )
    early_returned = [
        shifted(
            early_grad[:, WINDOW - distance * edge_rows : WINDOW - (distance - 1) * edge_rows],
            "seq",
            -distance,
        )
        for distance in range(1, far_blocks + 1)
    ]
    later_returned = [
        shifted(later_grad[:, (distance - 1) * edge_rows : distance * edge_rows], "seq", distance)
        for distance in range(1, far_blocks + 1)
    ]
    tail_extra = jnp.zeros((2, edge_rows, model_width), jnp.float32)
    for returned in early_returned:
        tail_extra = tail_extra + returned.astype(jnp.float32)
    head_extra = jnp.zeros((2, edge_rows, model_width), jnp.float32)
    for returned in later_returned:
        head_extra = head_extra + returned.astype(jnp.float32)
    own_grad = own_grad.at[:, rows_here - edge_rows :].add(tail_extra)
    own_grad = own_grad.at[:, :edge_rows].add(head_extra)
    grad_key = own_grad[0].astype(jnp.bfloat16)
    grad_value = own_grad[1].astype(jnp.bfloat16)
    return (layer_out[None], grad_query[None], grad_key[None], grad_value[None], grad_weight)


def solution(mesh):
    return jax.shard_map(
        body,
        mesh=mesh,
        in_specs=(
            P("doc", "seq", None),
            P("doc", "seq", None),
            P("doc", "seq", None),
            P("doc", "seq", None),
            P("doc", None),
            P("doc", None),
            P("doc", None),
        ),
        out_specs=(
            P("doc", "seq", None),
            P("doc", "seq", None),
            P("doc", "seq", None),
            P("doc", "seq", None),
            P("doc", None),
        ),
        check_vma=False,
    )
```

profile of v0, /device:TPU:2, one launch (start us, length us, event | category | flops | bytes accessed | tf_op | source)
XLA Modules:
  0.0 587.8 jit_solution(5047850334984720192)
XLA Ops:
  9.6 6.0 %collective-permute-start = (bf16[2,128,1024]{1,2,0:T(8,128)(2,1)S(1)}, bf16[2,128,1024]{1,2,0:T(8,128)(2,1)}, u32[]{:S(2)}, u32[]{:S(2)}) collective-permute-start(bf16[2,128,1024]{1,2,0:T(8,128)(2,1)S(1)} %pad_maximum_fusion.1), channel_id=1, source_target_pairs={{0,4},{1,5},{2,6},{3,7},{4,8},{5,9},{6,10},{7,11},{8,12},{9,13},{1... | collective-permute-start | bytes 1572872 | tf_op jit(solution)/shard_map/ppermute | solution.py:17
  15.5 4.9 collective-permute-start.1
  20.4 4.3 collective-permute-start.2
  24.7 3.7 collective-permute-start.3
  34.9 6.6 %collective-permute-done.1 = bf16[2,128,1024]{1,2,0:T(8,128)(2,1)S(1)} collective-permute-done((bf16[2,128,1024]{1,2,0:T(8,128)(2,1)S(1)}, bf16[2,128,1024]{1,2,0:T(8,128)(2,1)S(1)}, u32[]{:S(2)}, u32[]{:S(2)}) %collective-permute-start.1) | collective-permute-done | bytes 524320 | tf_op jit(solution)/shard_map/ppermute | solution.py:17
  42.9 8.7 %collective-permute-done.2 = bf16[2,128,1024]{1,2,0:T(8,128)(2,1)S(1)} collective-permute-done((bf16[2,128,1024]{1,2,0:T(8,128)(2,1)S(1)}, bf16[2,128,1024]{1,2,0:T(8,128)(2,1)S(1)}, u32[]{:S(2)}, u32[]{:S(2)}) %collective-permute-start.2) | collective-permute-done | bytes 524320 | tf_op jit(solution)/shard_map/ppermute | solution.py:17
  55.2 21.0 %collective-permute-done.6 = bf16[2,128,1024]{1,2,0:T(8,128)(2,1)S(1)} collective-permute-done((bf16[2,128,1024]{1,2,0:T(8,128)(2,1)S(1)}, bf16[2,128,1024]{1,2,0:T(8,128)(2,1)S(1)}, u32[]{:S(2)}, u32[]{:S(2)}) %collective-permute-start.6) | collective-permute-done | bytes 524320 | tf_op jit(solution)/shard_map/ppermute | solution.py:17
  76.3 30.6 %collective-permute-done.7 = bf16[2,128,1024]{1,2,0:T(8,128)(2,1)S(1)} collective-permute-done((bf16[2,128,1024]{1,2,0:T(8,128)(2,1)S(1)}, bf16[2,128,1024]{1,2,0:T(8,128)(2,1)S(1)}, u32[]{:S(2)}, u32[]{:S(2)}) %collective-permute-start.7) | collective-permute-done | bytes 524320 | tf_op jit(solution)/shard_map/ppermute | solution.py:17
  107.0 2.5 slice_bitcast_fusion
  109.6 29.0 %while.38 = (s32[]{:T(128)}, bf16[128,1024]{0,1:T(8,128)(2,1)S(1)}, bf16[1152,1024]{0,1:T(8,128)(2,1)}, bf16[128,1024]{0,1:T(8,128)(2,1)}, bf16[1152,1024]{0,1:T...) while((s32[]{:T(128)}, bf16[128,1024]{0,1:T(8,128)(2,1)S(1)}, ...), condition=%wide.region_6.7_spmd.clone, body=%wide.region_3.6_spmd.clone.sunk | while | flops 155452544 | bytes 8961351 | solution.py:93
  138.6 2.7 fusion.51
  141.7 3.1 convolution_convert_fusion
  149.8 94.7 %while.39 = (s32[]{:T(128)}, bf16[128,1024]{1,0:T(8,128)(2,1)}, f32[2,128,1024]{2,1,0:T(8,128)}, bf16[2,512,1024]{2,1,0:T(8,128)(2,1)}, bf16[2,512,1024]{2,1,0:T...) while((s32[]{:T(128)}, bf16[128,1024]{1,0:T(8,128)(2,1)}, ...), condition=%wide.region_12.13_spmd.clone, body=%wide.region_8.12_spmd.clone.sunk | while | flops 390861184 | bytes 38351472 | solution.py:157
  155.4 2.4 fusion.118
  157.8 4.7 fusion.119
  163.4 5.2 fusion.120
  181.8 4.7 fusion.119
  187.3 5.0 fusion.120
  205.4 4.7 fusion.119
  210.9 5.0 fusion.120
  226.5 2.4 fusion.118
  228.9 4.7 fusion.119
  234.4 5.2 fusion.120
  244.6 2.7 fusion.58
  247.3 11.6 %collective-permute-start.15 = (bf16[2,128,1024]{2,1,0:T(8,128)(2,1)S(1)}, bf16[2,128,1024]{2,1,0:T(8,128)(2,1)S(1)}, u32[]{:S(2)}, u32[]{:S(2)}) collective-permute-start(bf16[2,128,1024]{2,1,0:T(8,128)(2,1)S(1)} %get-tuple-element.488), channel_id=1, source_target_pairs={{0,4},{1,5},{2,6},{3,7},{4,8},{5,9},{6,10},{7,11},{8,12},{9,13},{1... | collective-permute-start | bytes 1572872 | tf_op jit(solution)/shard_map/ppermute | solution.py:17
  261.5 6.2 %collective-permute-start.12 = (bf16[2,128,1024]{2,1,0:T(8,128)(2,1)}, bf16[2,128,1024]{2,1,0:T(8,128)(2,1)S(1)}, u32[]{:S(2)}, u32[]{:S(2)}) collective-permute-start(bf16[2,128,1024]{2,1,0:T(8,128)(2,1)} %get-tuple-element.485), channel_id=1, source_target_pairs={{0,1},{1,2},{2,3},{3,4},{4,5},{5,6},{6,7},{7,8},{8,9},{9,10},{10,1... | collective-permute-start | bytes 1572872 | tf_op jit(solution)/shard_map/ppermute | solution.py:17
  272.4 10.0 %collective-permute-done.14 = bf16[2,128,1024]{2,1,0:T(8,128)(2,1)S(1)} collective-permute-done((bf16[2,128,1024]{2,1,0:T(8,128)(2,1)S(1)}, bf16[2,128,1024]{2,1,0:T(8,128)(2,1)S(1)}, u32[]{:S(2)}, u32[]{:S(2)}) %collective-permute-start.14) | collective-permute-done | bytes 524320 | tf_op jit(solution)/shard_map/ppermute | solution.py:17
  283.7 8.7 %collective-permute-done.13 = bf16[2,128,1024]{2,1,0:T(8,128)(2,1)S(1)} collective-permute-done((bf16[2,128,1024]{2,1,0:T(8,128)(2,1)S(1)}, bf16[2,128,1024]{2,1,0:T(8,128)(2,1)S(1)}, u32[]{:S(2)}, u32[]{:S(2)}) %collective-permute-start.13) | collective-permute-done | bytes 524320 | tf_op jit(solution)/shard_map/ppermute | solution.py:17
  294.9 6.7 %collective-permute-done.10 = bf16[2,128,1024]{2,1,0:T(8,128)(2,1)} collective-permute-done((bf16[2,128,1024]{2,1,0:T(8,128)(2,1)}, bf16[2,128,1024]{2,1,0:T(8,128)(2,1)}, u32[]{:S(2)}, u32[]{:S(2)}) %collective-permute-start.10) | collective-permute-done | bytes 524320 | tf_op jit(solution)/shard_map/ppermute | solution.py:17
  301.6 10.5 %collective-permute-done.9 = bf16[2,128,1024]{2,1,0:T(8,128)(2,1)} collective-permute-done((bf16[2,128,1024]{2,1,0:T(8,128)(2,1)}, bf16[2,128,1024]{2,1,0:T(8,128)(2,1)}, u32[]{:S(2)}, u32[]{:S(2)}) %collective-permute-start.9) | collective-permute-done | bytes 524320 | tf_op jit(solution)/shard_map/ppermute | solution.py:17
  312.6 2.4 add_convert_fusion
  315.9 263.7 %all-reduce.2.cloned.1.call-done = f32[64,1024]{1,0:T(8,128)} async-done(((f32[64,1024]{1,0:T(8,128)}), f32[64,1024]{1,0:T(8,128)}) %all-reduce.2.cloned.1.call-update) | async-done | bytes 262160 | tf_op jit(solution)/shard_map/psum | solution.py:108
  (241 shorter events, 112.0 us)
Async XLA Ops:
  7.2 24.3 %copy-start.8 = (bf16[1,128,1024]{2,1,0:T(8,128)(2,1)S(1)}, bf16[1,128,1024]{2,1,0:T(8,128)(2,1)}, u32[]{:S(2)}) copy-start(bf16[1,128,1024]{2,1,0:T(8,128)(2,1)} %param.19) | copy-start | bytes 786436
  7.2 134.5 %all-gather.2.cloned.1.call-start = ((), (), s32[]{:S(2)}) async-start(), calls=%async_computation.1 | async-start | bytes 2228224 | tf_op jit(solution)/shard_map/all_gather | solution.py:96
  9.6 22.9 %collective-permute-start = (bf16[2,128,1024]{1,2,0:T(8,128)(2,1)S(1)}, bf16[2,128,1024]{1,2,0:T(8,128)(2,1)}, u32[]{:S(2)}, u32[]{:S(2)}) collective-permute-start(bf16[2,128,1024]{1,2,0:T(8,128)(2,1)S(1)} %pad_maximum_fusion.1), channel_id=1, source_target_pairs={{0,4},{1,5},{2,6},{3,7},{4,8},{5,9},{6,10},{7,11},{8,12},{9,13},{1... | collective-permute-start | bytes 1572872 | tf_op jit(solution)/shard_map/ppermute | solution.py:17
  15.5 26.0 %collective-permute-start.1 = (bf16[2,128,1024]{1,2,0:T(8,128)(2,1)S(1)}, bf16[2,128,1024]{1,2,0:T(8,128)(2,1)S(1)}, u32[]{:S(2)}, u32[]{:S(2)}) collective-permute-start(bf16[2,128,1024]{1,2,0:T(8,128)(2,1)S(1)} %pad_maximum_fusion.1), channel_id=1, source_target_pairs={{0,3},{1,4},{2,5},{3,6},{4,7},{5,8},{6,9},{7,10},{8,11},{9,12},{10... | collective-permute-start | bytes 1572872 | tf_op jit(solution)/shard_map/ppermute | solution.py:17
  20.4 31.2 %collective-permute-start.2 = (bf16[2,128,1024]{1,2,0:T(8,128)(2,1)S(1)}, bf16[2,128,1024]{1,2,0:T(8,128)(2,1)S(1)}, u32[]{:S(2)}, u32[]{:S(2)}) collective-permute-start(bf16[2,128,1024]{1,2,0:T(8,128)(2,1)S(1)} %pad_maximum_fusion.1), channel_id=1, source_target_pairs={{0,2},{1,3},{2,4},{3,5},{4,6},{5,7},{6,8},{7,9},{8,10},{9,11},{10,... | collective-permute-start | bytes 1572872 | tf_op jit(solution)/shard_map/ppermute | solution.py:17
  24.7 28.3 %collective-permute-start.3 = (bf16[2,128,1024]{1,2,0:T(8,128)(2,1)S(1)}, bf16[2,128,1024]{1,2,0:T(8,128)(2,1)S(1)}, u32[]{:S(2)}, u32[]{:S(2)}) collective-permute-start(bf16[2,128,1024]{1,2,0:T(8,128)(2,1)S(1)} %pad_maximum_fusion.1), channel_id=1, source_target_pairs={{0,1},{1,2},{2,3},{3,4},{4,5},{5,6},{6,7},{7,8},{8,9},{9,10},{10,1... | collective-permute-start | bytes 1572872 | tf_op jit(solution)/shard_map/ppermute | solution.py:17
  28.4 24.9 %collective-permute-start.4 = (bf16[2,128,1024]{1,2,0:T(8,128)(2,1)S(1)}, bf16[2,128,1024]{1,2,0:T(8,128)(2,1)S(1)}, u32[]{:S(2)}, u32[]{:S(2)}) collective-permute-start(bf16[2,128,1024]{1,2,0:T(8,128)(2,1)S(1)} %pad_maximum_fusion.1), channel_id=1, source_target_pairs={{1,0},{2,1},{3,2},{4,3},{5,4},{6,5},{7,6},{8,7},{9,8},{10,9},{11,1... | collective-permute-start | bytes 1572872 | tf_op jit(solution)/shard_map/ppermute | solution.py:17
  29.7 265.1 %reduce-scatter.2.cloned.1.call-start = ((), (), s32[]{:S(2)}) async-start(), calls=%async_computation.2 | async-start | bytes 4456448 | tf_op jit(solution)/shard_map/reduce_scatter | solution.py:107
  32.4 22.7 %collective-permute-start.5 = (bf16[2,128,1024]{1,2,0:T(8,128)(2,1)S(1)}, bf16[2,128,1024]{1,2,0:T(8,128)(2,1)S(1)}, u32[]{:S(2)}, u32[]{:S(2)}) collective-permute-start(bf16[2,128,1024]{1,2,0:T(8,128)(2,1)S(1)} %pad_maximum_fusion.1), channel_id=1, source_target_pairs={{2,0},{3,1},{4,2},{5,3},{6,4},{7,5},{8,6},{9,7},{10,8},{11,9},{12,... | collective-permute-start | bytes 1572872 | tf_op jit(solution)/shard_map/ppermute | solution.py:17
  41.5 34.7 %collective-permute-start.6 = (bf16[2,128,1024]{1,2,0:T(8,128)(2,1)S(1)}, bf16[2,128,1024]{1,2,0:T(8,128)(2,1)S(1)}, u32[]{:S(2)}, u32[]{:S(2)}) collective-permute-start(bf16[2,128,1024]{1,2,0:T(8,128)(2,1)S(1)} %pad_maximum_fusion.1), channel_id=1, source_target_pairs={{3,0},{4,1},{5,2},{6,3},{7,4},{8,5},{9,6},{10,7},{11,8},{12,9},{13... | collective-permute-start | bytes 1572872 | tf_op jit(solution)/shard_map/ppermute | solution.py:17
  51.6 55.3 %collective-permute-start.7 = (bf16[2,128,1024]{1,2,0:T(8,128)(2,1)S(1)}, bf16[2,128,1024]{1,2,0:T(8,128)(2,1)S(1)}, u32[]{:S(2)}, u32[]{:S(2)}) collective-permute-start(bf16[2,128,1024]{1,2,0:T(8,128)(2,1)S(1)} %pad_maximum_fusion.1), channel_id=1, source_target_pairs={{4,0},{5,1},{6,2},{7,3},{8,4},{9,5},{10,6},{11,7},{12,8},{13,9},{1... | collective-permute-start | bytes 1572872 | tf_op jit(solution)/shard_map/ppermute | solution.py:17
  109.6 29.0 %copy-start.7 = (bf16[1,128,1024]{2,1,0:T(8,128)(2,1)S(1)}, bf16[1,128,1024]{2,1,0:T(8,128)(2,1)}, u32[]{:S(2)}) copy-start(bf16[1,128,1024]{2,1,0:T(8,128)(2,1)} %param.22) | copy-start | bytes 786436
  141.4 438.2 %all-reduce.2.cloned.1.call-start = ((), (), s32[]{:S(2)}) async-start(), calls=%async_computation.3 | async-start | bytes 524288 | tf_op jit(solution)/shard_map/psum | solution.py:108
  151.9 10.7 %copy-start.2 = (bf16[128,256]{0,1:T(8,128)(2,1)}, bf16[128,256]{0,1:T(8,128)(2,1)S(1)}, u32[]{:S(2)}) copy-start(bf16[128,256]{0,1:T(8,128)(2,1)S(1)} %copy.54) | copy-start | bytes 196612 | tf_op jit(solution)/shard_map/while
  154.5 8.1 %copy-start.6 = (bf16[128,256]{0,1:T(8,128)(2,1)}, bf16[128,256]{0,1:T(8,128)(2,1)S(1)}, u32[]{:S(2)}) copy-start(bf16[128,256]{0,1:T(8,128)(2,1)S(1)} %constant_dynamic-slice_fusion.18) | copy-start | bytes 196612 | tf_op jit(solution)/shard_map/while
  175.9 10.7 %copy-start.2 = (bf16[128,256]{0,1:T(8,128)(2,1)}, bf16[128,256]{0,1:T(8,128)(2,1)S(1)}, u32[]{:S(2)}) copy-start(bf16[128,256]{0,1:T(8,128)(2,1)S(1)} %copy.54) | copy-start | bytes 196612 | tf_op jit(solution)/shard_map/while
  178.4 8.1 %copy-start.6 = (bf16[128,256]{0,1:T(8,128)(2,1)}, bf16[128,256]{0,1:T(8,128)(2,1)S(1)}, u32[]{:S(2)}) copy-start(bf16[128,256]{0,1:T(8,128)(2,1)S(1)} %constant_dynamic-slice_fusion.18) | copy-start | bytes 196612 | tf_op jit(solution)/shard_map/while
  199.4 10.7 %copy-start.2 = (bf16[128,256]{0,1:T(8,128)(2,1)}, bf16[128,256]{0,1:T(8,128)(2,1)S(1)}, u32[]{:S(2)}) copy-start(bf16[128,256]{0,1:T(8,128)(2,1)S(1)} %copy.54) | copy-start | bytes 196612 | tf_op jit(solution)/shard_map/while
  223.0 10.7 %copy-start.2 = (bf16[128,256]{0,1:T(8,128)(2,1)}, bf16[128,256]{0,1:T(8,128)(2,1)S(1)}, u32[]{:S(2)}) copy-start(bf16[128,256]{0,1:T(8,128)(2,1)S(1)} %copy.54) | copy-start | bytes 196612 | tf_op jit(solution)/shard_map/while
  225.5 8.1 %copy-start.6 = (bf16[128,256]{0,1:T(8,128)(2,1)}, bf16[128,256]{0,1:T(8,128)(2,1)S(1)}, u32[]{:S(2)}) copy-start(bf16[128,256]{0,1:T(8,128)(2,1)S(1)} %constant_dynamic-slice_fusion.18) | copy-start | bytes 196612 | tf_op jit(solution)/shard_map/while
  244.6 23.1 %copy-start.1 = (bf16[2,512,1024]{2,1,0:T(8,128)(2,1)S(1)}, bf16[2,512,1024]{2,1,0:T(8,128)(2,1)}, u32[]{:S(2)}) copy-start(bf16[2,512,1024]{2,1,0:T(8,128)(2,1)} %get-tuple-element.329) | copy-start | bytes 6291460
  247.3 46.4 %copy-start = (bf16[1024,1024]{1,0:T(8,128)(2,1)S(1)}, bf16[1024,1024]{1,0:T(8,128)(2,1)}, u32[]{:S(2)}) copy-start(bf16[1024,1024]{1,0:T(8,128)(2,1)} %all-gather.2.cloned.1.call-done) | copy-start | bytes 6291460
  247.3 46.4 %copy-start.5 = (bf16[128,1024]{0,1:T(8,128)(2,1)S(1)}, bf16[128,1024]{0,1:T(8,128)(2,1)}, u32[]{:S(2)}) copy-start(bf16[128,1024]{0,1:T(8,128)(2,1)} %copy-done.4) | copy-start | bytes 786436
  247.3 23.9 %collective-permute-start.15 = (bf16[2,128,1024]{2,1,0:T(8,128)(2,1)S(1)}, bf16[2,128,1024]{2,1,0:T(8,128)(2,1)S(1)}, u32[]{:S(2)}, u32[]{:S(2)}) collective-permute-start(bf16[2,128,1024]{2,1,0:T(8,128)(2,1)S(1)} %get-tuple-element.488), channel_id=1, source_target_pairs={{0,4},{1,5},{2,6},{3,7},{4,8},{5,9},{6,10},{7,11},{8,12},{9,13},{1... | collective-permute-start | bytes 1572872 | tf_op jit(solution)/shard_map/ppermute | solution.py:17
  258.8 23.6 %collective-permute-start.14 = (bf16[2,128,1024]{2,1,0:T(8,128)(2,1)S(1)}, bf16[2,128,1024]{2,1,0:T(8,128)(2,1)S(1)}, u32[]{:S(2)}, u32[]{:S(2)}) collective-permute-start(bf16[2,128,1024]{2,1,0:T(8,128)(2,1)S(1)} %get-tuple-element.486), channel_id=1, source_target_pairs={{0,3},{1,4},{2,5},{3,6},{4,7},{5,8},{6,9},{7,10},{8,11},{9,12},{10... | collective-permute-start | bytes 1572872 | tf_op jit(solution)/shard_map/ppermute | solution.py:17
  260.2 32.2 %collective-permute-start.13 = (bf16[2,128,1024]{2,1,0:T(8,128)(2,1)S(1)}, bf16[2,128,1024]{2,1,0:T(8,128)(2,1)S(1)}, u32[]{:S(2)}, u32[]{:S(2)}) collective-permute-start(bf16[2,128,1024]{2,1,0:T(8,128)(2,1)S(1)} %get-tuple-element.487), channel_id=1, source_target_pairs={{0,2},{1,3},{2,4},{3,5},{4,6},{5,7},{6,8},{7,9},{8,10},{9,11},{10,... | collective-permute-start | bytes 1572872 | tf_op jit(solution)/shard_map/ppermute | solution.py:17
  261.5 33.4 %collective-permute-start.12 = (bf16[2,128,1024]{2,1,0:T(8,128)(2,1)}, bf16[2,128,1024]{2,1,0:T(8,128)(2,1)S(1)}, u32[]{:S(2)}, u32[]{:S(2)}) collective-permute-start(bf16[2,128,1024]{2,1,0:T(8,128)(2,1)} %get-tuple-element.485), channel_id=1, source_target_pairs={{0,1},{1,2},{2,3},{3,4},{4,5},{5,6},{6,7},{7,8},{8,9},{9,10},{10,1... | collective-permute-start | bytes 1572872 | tf_op jit(solution)/shard_map/ppermute | solution.py:17
  269.0 43.6 %copy-start.3 = (f32[2,128,1024]{2,1,0:T(8,128)S(1)}, f32[2,128,1024]{2,1,0:T(8,128)}, u32[]{:S(2)}) copy-start(f32[2,128,1024]{2,1,0:T(8,128)} %get-tuple-element.328) | copy-start | bytes 3145732
  269.0 25.9 %collective-permute-start.11 = (bf16[2,128,1024]{2,1,0:T(8,128)(2,1)}, bf16[2,128,1024]{2,1,0:T(8,128)(2,1)}, u32[]{:S(2)}, u32[]{:S(2)}) collective-permute-start(bf16[2,128,1024]{2,1,0:T(8,128)(2,1)} %get-tuple-element.484), channel_id=1, source_target_pairs={{4,0},{5,1},{6,2},{7,3},{8,4},{9,5},{10,6},{11,7},{12,8},{13,9},{1... | collective-permute-start | bytes 1572872 | tf_op jit(solution)/shard_map/ppermute | solution.py:17
  271.1 30.4 %collective-permute-start.10 = (bf16[2,128,1024]{2,1,0:T(8,128)(2,1)}, bf16[2,128,1024]{2,1,0:T(8,128)(2,1)}, u32[]{:S(2)}, u32[]{:S(2)}) collective-permute-start(bf16[2,128,1024]{2,1,0:T(8,128)(2,1)} %get-tuple-element.482), channel_id=1, source_target_pairs={{3,0},{4,1},{5,2},{6,3},{7,4},{8,5},{9,6},{10,7},{11,8},{12,9},{13... | collective-permute-start | bytes 1572872 | tf_op jit(solution)/shard_map/ppermute | solution.py:17
  282.4 29.6 %collective-permute-start.9 = (bf16[2,128,1024]{2,1,0:T(8,128)(2,1)}, bf16[2,128,1024]{2,1,0:T(8,128)(2,1)}, u32[]{:S(2)}, u32[]{:S(2)}) collective-permute-start(bf16[2,128,1024]{2,1,0:T(8,128)(2,1)} %get-tuple-element.483), channel_id=1, source_target_pairs={{2,0},{3,1},{4,2},{5,3},{6,4},{7,5},{8,6},{9,7},{10,8},{11,9},{12,... | collective-permute-start | bytes 1572872 | tf_op jit(solution)/shard_map/ppermute | solution.py:17
  292.4 20.2 %collective-permute-start.8 = (bf16[2,128,1024]{2,1,0:T(8,128)(2,1)}, bf16[2,128,1024]{2,1,0:T(8,128)(2,1)}, u32[]{:S(2)}, u32[]{:S(2)}) collective-permute-start(bf16[2,128,1024]{2,1,0:T(8,128)(2,1)} %get-tuple-element.481), channel_id=1, source_target_pairs={{1,0},{2,1},{3,2},{4,3},{5,4},{6,5},{7,6},{8,7},{9,8},{10,9},{11,1... | collective-permute-start | bytes 1572872 | tf_op jit(solution)/shard_map/ppermute | solution.py:17
  (30 other events, 88.4 us)
Sparse Core Ops, SparseCore 0:
  29.9 76.8 all-gather.1
  141.5 109.0 reduce-scatter.1
  295.0 284.5 all-reduce.1
where the time goes:
time: 590 us; the launch traced here: 588 us
  waiting for transfers between devices  369 us (63%)
  matrix products  85.4 us (14%)
  local copies, waits for them, and re-layouts  56 us (9%)
  starting transfers between devices  49.9 us (8%)
  between operations  14.1 us (2%)
  other arithmetic  12.1 us (2%)
    psum x1, waiting for transfers between devices, body(): weight_sum = lax.psum(row_block, 'seq')  264 us
    ppermute x16, waiting for transfers between devices, shifted(): lax.ppermute(value, axis, [(source, source + steps) for source in range(f...  106 us
    ppermute x16, starting transfers between devices, shifted(): lax.ppermute(value, axis, [(source, source + steps) for source in range(f...  49.6 us
    dot_general x4, matrix products, backward_group(): jnp.einsum('hqk,qhd->khd', grad_score, query_grp, preferred_element_type=...  20.5 us
    sub x8, matrix products, soft_weights(): exponent = jnp.exp(scores - row_peak)  19 us
    dot_general x4, matrix products, backward_group(): jnp.einsum('hqk,khd->qhd', grad_score, key_grp, preferred_element_type=jn...  19 us
  transfers between devices with their start and end apart: 19, of which 12 were waited for; matrix products, arithmetic and copies ran while one was open for 25% of the time, Pallas kernels for 0%

commit v1 on v0

--- a/solution.py
+++ b/solution.py
@@ -1,3 +1,4 @@
+import functools
 import math
 import jax
 import jax.numpy as jnp
@@ -9,6 +10,14 @@
 WINDOW = 512
 BLOCK = 64
 DOCS = 4
+
+
+def put_heads(field_in, chip_axis):
+    prior = jnp.sum(jax.lax.all_gather(field_in, axis_name=chip_axis), axis=0)
+    return prior
+
+
+order_strings_here = functools.partial(put_heads, chip_axis="seq")
 
 
 def shifted(value, axis, steps):
@@ -105,7 +114,7 @@
         attended, grad_out, (((0,), (0,)), ((), ())), preferred_element_type=jnp.float32
     )
     row_block = lax.psum_scatter(partial_grad, "doc", scatter_dimension=0, tiled=True)
-    weight_sum = lax.psum(row_block, "seq")
+    weight_sum = order_strings_here(row_block)
     grad_weight = weight_sum * (1.0 / math.sqrt(rows_here * seq_count * doc_count))
 
     def backward_group(group_index, grad_state):

time: 590 us -> 522 us (0.88)
  the two profiles are of different devices: /device:TPU:2 before, /device:TPU:94 now
where the time goes in v1:
time: 522 us; the launch traced here: 520 us
  waiting for transfers between devices  265 us (51%)
  starting transfers between devices  87.2 us (17%)
  matrix products  84.7 us (16%)
  local copies, waits for them, and re-layouts  54 us (10%)
  between operations  14.2 us (3%)
  other arithmetic  13.6 us (3%)
    ppermute x16, waiting for transfers between devices, shifted(): lax.ppermute(value, axis, [(source, source + steps) for source in range(f...  127 us
    reduce_scatter x1, waiting for transfers between devices, body(): lax.psum_scatter(partial_grad, 'doc', scatter_dimension=0, tiled=True)  108 us
    ppermute x16, starting transfers between devices, shifted(): lax.ppermute(value, axis, [(source, source + steps) for source in range(f...  86.9 us
    all_gather x1, waiting for transfers between devices, put_heads(): prior = jnp.sum(jax.lax.all_gather(field_in, axis_name=chip_axis), axis=0)  30.2 us
    dot_general x4, matrix products, backward_group(): jnp.einsum('hqk,qhd->khd', grad_score, query_grp, preferred_element_type=...  20.1 us
    dot_general x4, matrix products, backward_group(): jnp.einsum('hqk,khd->qhd', grad_score, key_grp, preferred_element_type=jn...  19.1 us
    sub x8, matrix products, soft_weights(): exponent = jnp.exp(scores - row_peak)  18.8 us
  transfers between devices with their start and end apart: 19, of which 11 were waited for; matrix products, arithmetic and copies ran while one was open for 28% of the time, Pallas kernels for 0%

profile of v1, /device:TPU:94, one launch (start us, length us, event | category | flops | bytes accessed | tf_op | source)
XLA Modules:
  0.0 519.9 jit_solution(17007499207706110030)
XLA Ops:
  9.6 6.4 %collective-permute-start = (bf16[2,128,1024]{1,2,0:T(8,128)(2,1)S(1)}, bf16[2,128,1024]{1,2,0:T(8,128)(2,1)}, u32[]{:S(2)}, u32[]{:S(2)}) collective-permute-start(bf16[2,128,1024]{1,2,0:T(8,128)(2,1)S(1)} %pad_maximum_fusion.1), channel_id=1, source_target_pairs={{0,4},{1,5},{2,6},{3,7},{4,8},{5,9},{6,10},{7,11},{8,12},{9,13},{1... | collective-permute-start | bytes 1572872 | tf_op jit(solution)/shard_map/ppermute | solution.py:26
  16.0 5.4 %collective-permute-start.1 = (bf16[2,128,1024]{1,2,0:T(8,128)(2,1)S(1)}, bf16[2,128,1024]{1,2,0:T(8,128)(2,1)S(1)}, u32[]{:S(2)}, u32[]{:S(2)}) collective-permute-start(bf16[2,128,1024]{1,2,0:T(8,128)(2,1)S(1)} %pad_maximum_fusion.1), channel_id=1, source_target_pairs={{0,3},{1,4},{2,5},{3,6},{4,7},{5,8},{6,9},{7,10},{8,11},{9,12},{10... | collective-permute-start | bytes 1572872 | tf_op jit(solution)/shard_map/ppermute | solution.py:26
  21.3 3.8 collective-permute-start.2
  25.2 3.2 collective-permute-start.3
  33.7 16.3 %collective-permute-start.5 = (bf16[2,128,1024]{1,2,0:T(8,128)(2,1)S(1)}, bf16[2,128,1024]{1,2,0:T(8,128)(2,1)S(1)}, u32[]{:S(2)}, u32[]{:S(2)}) collective-permute-start(bf16[2,128,1024]{1,2,0:T(8,128)(2,1)S(1)} %pad_maximum_fusion.1), channel_id=1, source_target_pairs={{2,0},{3,1},{4,2},{5,3},{6,4},{7,5},{8,6},{9,7},{10,8},{11,9},{12,... | collective-permute-start | bytes 1572872 | tf_op jit(solution)/shard_map/ppermute | solution.py:26
  51.2 10.7 %collective-permute-done.1 = bf16[2,128,1024]{1,2,0:T(8,128)(2,1)S(1)} collective-permute-done((bf16[2,128,1024]{1,2,0:T(8,128)(2,1)S(1)}, bf16[2,128,1024]{1,2,0:T(8,128)(2,1)S(1)}, u32[]{:S(2)}, u32[]{:S(2)}) %collective-permute-start.1) | collective-permute-done | bytes 524320 | tf_op jit(solution)/shard_map/ppermute | solution.py:26
  64.0 9.2 %collective-permute-done.2 = bf16[2,128,1024]{1,2,0:T(8,128)(2,1)S(1)} collective-permute-done((bf16[2,128,1024]{1,2,0:T(8,128)(2,1)S(1)}, bf16[2,128,1024]{1,2,0:T(8,128)(2,1)S(1)}, u32[]{:S(2)}, u32[]{:S(2)}) %collective-permute-start.2) | collective-permute-done | bytes 524320 | tf_op jit(solution)/shard_map/ppermute | solution.py:26
  75.2 12.7 %collective-permute-done.3 = bf16[2,128,1024]{1,2,0:T(8,128)(2,1)S(1)} collective-permute-done((bf16[2,128,1024]{1,2,0:T(8,128)(2,1)S(1)}, bf16[2,128,1024]{1,2,0:T(8,128)(2,1)S(1)}, u32[]{:S(2)}, u32[]{:S(2)}) %collective-permute-start.3) | collective-permute-done | bytes 524320 | tf_op jit(solution)/shard_map/ppermute | solution.py:26
  88.5 13.9 %collective-permute-done.6 = bf16[2,128,1024]{1,2,0:T(8,128)(2,1)S(1)} collective-permute-done((bf16[2,128,1024]{1,2,0:T(8,128)(2,1)S(1)}, bf16[2,128,1024]{1,2,0:T(8,128)(2,1)S(1)}, u32[]{:S(2)}, u32[]{:S(2)}) %collective-permute-start.6) | collective-permute-done | bytes 524320 | tf_op jit(solution)/shard_map/ppermute | solution.py:26
  105.2 29.0 %while.38 = (s32[]{:T(128)}, bf16[128,1024]{0,1:T(8,128)(2,1)S(1)}, bf16[1152,1024]{0,1:T(8,128)(2,1)}, bf16[128,1024]{0,1:T(8,128)(2,1)}, bf16[1152,1024]{0,1:T...) while((s32[]{:T(128)}, bf16[128,1024]{0,1:T(8,128)(2,1)S(1)}, ...), condition=%wide.region_6.7_spmd.clone, body=%wide.region_3.6_spmd.clone.sunk | while | flops 155452544 | bytes 8961351 | solution.py:102
  140.4 107.6 %reduce-scatter.2.cloned.1.call-done = f32[64,1024]{1,0:T(8,128)} async-done(((f32[1024,1024]{1,0:T(8,128)}), f32[64,1024]{1,0:T(8,128)}) %reduce-scatter.2.cloned.1.call-update) | async-done | bytes 262160 | tf_op jit(solution)/shard_map/reduce_scatter | solution.py:116
  253.1 93.9 %while.39 = (s32[]{:T(128)}, bf16[128,1024]{1,0:T(8,128)(2,1)}, f32[2,128,1024]{2,1,0:T(8,128)}, bf16[2,512,1024]{2,1,0:T(8,128)(2,1)}, bf16[2,512,1024]{2,1,0:T...) while((s32[]{:T(128)}, bf16[128,1024]{1,0:T(8,128)(2,1)}, ...), condition=%wide.region_12.13_spmd.clone, body=%wide.region_8.12_spmd.clone.sunk | while | flops 390861184 | bytes 38351472 | solution.py:166
  261.0 4.7 fusion.119
  266.6 5.1 fusion.120
  284.6 4.8 fusion.119
  290.1 5.0 fusion.120
  308.1 4.8 fusion.119
  313.6 5.0 fusion.120
  331.5 4.8 fusion.119
  337.0 5.0 fusion.120
  348.9 5.8 %collective-permute-start.15 = (bf16[2,128,1024]{2,1,0:T(8,128)(2,1)S(1)}, bf16[2,128,1024]{2,1,0:T(8,128)(2,1)S(1)}, u32[]{:S(2)}, u32[]{:S(2)}) collective-permute-start(bf16[2,128,1024]{2,1,0:T(8,128)(2,1)S(1)} %get-tuple-element.488), channel_id=1, source_target_pairs={{0,4},{1,5},{2,6},{3,7},{4,8},{5,9},{6,10},{7,11},{8,12},{9,13},{1... | collective-permute-start | bytes 1572872 | tf_op jit(solution)/shard_map/ppermute | solution.py:26
  354.7 3.6 collective-permute-start.14
  358.3 3.4 collective-permute-start.13
  361.7 4.3 collective-permute-start.12
  368.7 8.6 %collective-permute-done.15 = bf16[2,128,1024]{2,1,0:T(8,128)(2,1)S(1)} collective-permute-done((bf16[2,128,1024]{2,1,0:T(8,128)(2,1)S(1)}, bf16[2,128,1024]{2,1,0:T(8,128)(2,1)S(1)}, u32[]{:S(2)}, u32[]{:S(2)}) %collective-permute-start.15) | collective-permute-done | bytes 524320 | tf_op jit(solution)/shard_map/ppermute | solution.py:26
  379.2 16.6 %collective-permute-done.14 = bf16[2,128,1024]{2,1,0:T(8,128)(2,1)S(1)} collective-permute-done((bf16[2,128,1024]{2,1,0:T(8,128)(2,1)S(1)}, bf16[2,128,1024]{2,1,0:T(8,128)(2,1)S(1)}, u32[]{:S(2)}, u32[]{:S(2)}) %collective-permute-start.14) | collective-permute-done | bytes 524320 | tf_op jit(solution)/shard_map/ppermute | solution.py:26
  395.8 22.0 %collective-permute-start.9 = (bf16[2,128,1024]{2,1,0:T(8,128)(2,1)S(1)}, bf16[2,128,1024]{2,1,0:T(8,128)(2,1)S(1)}, u32[]{:S(2)}, u32[]{:S(2)}) collective-permute-start(bf16[2,128,1024]{2,1,0:T(8,128)(2,1)S(1)} %get-tuple-element.483), channel_id=1, source_target_pairs={{2,0},{3,1},{4,2},{5,3},{6,4},{7,5},{8,6},{9,7},{10,8},{11,9},{12,... | collective-permute-start | bytes 1572872 | tf_op jit(solution)/shard_map/ppermute | solution.py:26
  417.8 18.2 %collective-permute-done.13 = bf16[2,128,1024]{2,1,0:T(8,128)(2,1)S(1)} collective-permute-done((bf16[2,128,1024]{2,1,0:T(8,128)(2,1)S(1)}, bf16[2,128,1024]{2,1,0:T(8,128)(2,1)S(1)}, u32[]{:S(2)}, u32[]{:S(2)}) %collective-permute-start.13) | collective-permute-done | bytes 524320 | tf_op jit(solution)/shard_map/ppermute | solution.py:26
  439.2 10.7 %collective-permute-done.12 = bf16[2,128,1024]{2,1,0:T(8,128)(2,1)S(1)} collective-permute-done((bf16[2,128,1024]{2,1,0:T(8,128)(2,1)S(1)}, bf16[2,128,1024]{2,1,0:T(8,128)(2,1)S(1)}, u32[]{:S(2)}, u32[]{:S(2)}) %collective-permute-start.12) | collective-permute-done | bytes 524320 | tf_op jit(solution)/shard_map/ppermute | solution.py:26
  449.9 26.8 %collective-permute-done.8 = bf16[2,128,1024]{2,1,0:T(8,128)(2,1)S(1)} collective-permute-done((bf16[2,128,1024]{2,1,0:T(8,128)(2,1)S(1)}, bf16[2,128,1024]{2,1,0:T(8,128)(2,1)S(1)}, u32[]{:S(2)}, u32[]{:S(2)}) %collective-permute-start.8) | collective-permute-done | bytes 524320 | tf_op jit(solution)/shard_map/ppermute | solution.py:26
  478.5 30.2 %all-gather.6.cloned.1.call-done = f32[2048,1024]{1,0:T(8,128)} async-done(((f32[64,1024]{1,0:T(8,128)}), f32[2048,1024]{1,0:T(8,128)}) %all-gather.6.cloned.1.call-update) | async-done | bytes 8388624 | tf_op jit(solution)/shard_map/all_gather | solution.py:16
  508.7 4.0 reduce_sum.78
  (242 shorter events, 122.2 us)
Async XLA Ops:
  7.2 25.6 %copy-start.8 = (bf16[1,128,1024]{2,1,0:T(8,128)(2,1)S(1)}, bf16[1,128,1024]{2,1,0:T(8,128)(2,1)}, u32[]{:S(2)}) copy-start(bf16[1,128,1024]{2,1,0:T(8,128)(2,1)} %param.19) | copy-start | bytes 786436
  7.2 130.1 %all-gather.4.cloned.1.call-start = ((), (), s32[]{:S(2)}) async-start(), calls=%async_computation.1 | async-start | bytes 2228224 | tf_op jit(solution)/shard_map/all_gather | solution.py:105
  9.6 24.2 %collective-permute-start = (bf16[2,128,1024]{1,2,0:T(8,128)(2,1)S(1)}, bf16[2,128,1024]{1,2,0:T(8,128)(2,1)}, u32[]{:S(2)}, u32[]{:S(2)}) collective-permute-start(bf16[2,128,1024]{1,2,0:T(8,128)(2,1)S(1)} %pad_maximum_fusion.1), channel_id=1, source_target_pairs={{0,4},{1,5},{2,6},{3,7},{4,8},{5,9},{6,10},{7,11},{8,12},{9,13},{1... | collective-permute-start | bytes 1572872 | tf_op jit(solution)/shard_map/ppermute | solution.py:26
  16.0 46.0 %collective-permute-start.1 = (bf16[2,128,1024]{1,2,0:T(8,128)(2,1)S(1)}, bf16[2,128,1024]{1,2,0:T(8,128)(2,1)S(1)}, u32[]{:S(2)}, u32[]{:S(2)}) collective-permute-start(bf16[2,128,1024]{1,2,0:T(8,128)(2,1)S(1)} %pad_maximum_fusion.1), channel_id=1, source_target_pairs={{0,3},{1,4},{2,5},{3,6},{4,7},{5,8},{6,9},{7,10},{8,11},{9,12},{10... | collective-permute-start | bytes 1572872 | tf_op jit(solution)/shard_map/ppermute | solution.py:26
  21.3 51.8 %collective-permute-start.2 = (bf16[2,128,1024]{1,2,0:T(8,128)(2,1)S(1)}, bf16[2,128,1024]{1,2,0:T(8,128)(2,1)S(1)}, u32[]{:S(2)}, u32[]{:S(2)}) collective-permute-start(bf16[2,128,1024]{1,2,0:T(8,128)(2,1)S(1)} %pad_maximum_fusion.1), channel_id=1, source_target_pairs={{0,2},{1,3},{2,4},{3,5},{4,6},{5,7},{6,8},{7,9},{8,10},{9,11},{10,... | collective-permute-start | bytes 1572872 | tf_op jit(solution)/shard_map/ppermute | solution.py:26
  25.2 62.7 %collective-permute-start.3 = (bf16[2,128,1024]{1,2,0:T(8,128)(2,1)S(1)}, bf16[2,128,1024]{1,2,0:T(8,128)(2,1)S(1)}, u32[]{:S(2)}, u32[]{:S(2)}) collective-permute-start(bf16[2,128,1024]{1,2,0:T(8,128)(2,1)S(1)} %pad_maximum_fusion.1), channel_id=1, source_target_pairs={{0,1},{1,2},{2,3},{3,4},{4,5},{5,6},{6,7},{7,8},{8,9},{9,10},{10,1... | collective-permute-start | bytes 1572872 | tf_op jit(solution)/shard_map/ppermute | solution.py:26
  28.4 59.8 %collective-permute-start.4 = (bf16[2,128,1024]{1,2,0:T(8,128)(2,1)S(1)}, bf16[2,128,1024]{1,2,0:T(8,128)(2,1)S(1)}, u32[]{:S(2)}, u32[]{:S(2)}) collective-permute-start(bf16[2,128,1024]{1,2,0:T(8,128)(2,1)S(1)} %pad_maximum_fusion.1), channel_id=1, source_target_pairs={{1,0},{2,1},{3,2},{4,3},{5,4},{6,5},{7,6},{8,7},{9,8},{10,9},{11,1... | collective-permute-start | bytes 1572872 | tf_op jit(solution)/shard_map/ppermute | solution.py:26
  31.0 216.9 %reduce-scatter.2.cloned.1.call-start = ((), (), s32[]{:S(2)}) async-start(), calls=%async_computation.2 | async-start | bytes 4456448 | tf_op jit(solution)/shard_map/reduce_scatter | solution.py:116
  33.7 54.6 %collective-permute-start.5 = (bf16[2,128,1024]{1,2,0:T(8,128)(2,1)S(1)}, bf16[2,128,1024]{1,2,0:T(8,128)(2,1)S(1)}, u32[]{:S(2)}, u32[]{:S(2)}) collective-permute-start(bf16[2,128,1024]{1,2,0:T(8,128)(2,1)S(1)} %pad_maximum_fusion.1), channel_id=1, source_target_pairs={{2,0},{3,1},{4,2},{5,3},{6,4},{7,5},{8,6},{9,7},{10,8},{11,9},{12,... | collective-permute-start | bytes 1572872 | tf_op jit(solution)/shard_map/ppermute | solution.py:26
  61.9 40.4 %collective-permute-start.6 = (bf16[2,128,1024]{1,2,0:T(8,128)(2,1)S(1)}, bf16[2,128,1024]{1,2,0:T(8,128)(2,1)S(1)}, u32[]{:S(2)}, u32[]{:S(2)}) collective-permute-start(bf16[2,128,1024]{1,2,0:T(8,128)(2,1)S(1)} %pad_maximum_fusion.1), channel_id=1, source_target_pairs={{3,0},{4,1},{5,2},{6,3},{7,4},{8,5},{9,6},{10,7},{11,8},{12,9},{13... | collective-permute-start | bytes 1572872 | tf_op jit(solution)/shard_map/ppermute | solution.py:26
  73.2 29.3 %collective-permute-start.7 = (bf16[2,128,1024]{1,2,0:T(8,128)(2,1)S(1)}, bf16[2,128,1024]{1,2,0:T(8,128)(2,1)S(1)}, u32[]{:S(2)}, u32[]{:S(2)}) collective-permute-start(bf16[2,128,1024]{1,2,0:T(8,128)(2,1)S(1)} %pad_maximum_fusion.1), channel_id=1, source_target_pairs={{4,0},{5,1},{6,2},{7,3},{8,4},{9,5},{10,6},{11,7},{12,8},{13,9},{1... | collective-permute-start | bytes 1572872 | tf_op jit(solution)/shard_map/ppermute | solution.py:26
  105.2 29.0 %copy-start.7 = (bf16[1,128,1024]{2,1,0:T(8,128)(2,1)S(1)}, bf16[1,128,1024]{2,1,0:T(8,128)(2,1)}, u32[]{:S(2)}) copy-start(bf16[1,128,1024]{2,1,0:T(8,128)(2,1)} %param.22) | copy-start | bytes 786436
  137.0 371.7 %all-gather.6.cloned.1.call-start = ((), (), s32[]{:S(2)}) async-start(), calls=%async_computation.3 | async-start | bytes 8650752 | tf_op jit(solution)/shard_map/all_gather | solution.py:16
  257.7 8.0 %copy-start.6 = (bf16[128,256]{0,1:T(8,128)(2,1)}, bf16[128,256]{0,1:T(8,128)(2,1)S(1)}, u32[]{:S(2)}) copy-start(bf16[128,256]{0,1:T(8,128)(2,1)S(1)} %constant_dynamic-slice_fusion.18) | copy-start | bytes 196612 | tf_op jit(solution)/shard_map/while
  278.7 5.9 %copy-start.2 = (bf16[128,256]{0,1:T(8,128)(2,1)}, bf16[128,256]{0,1:T(8,128)(2,1)S(1)}, u32[]{:S(2)}) copy-start(bf16[128,256]{0,1:T(8,128)(2,1)S(1)} %copy.55) | copy-start | bytes 196612 | tf_op jit(solution)/shard_map/while
  281.3 8.1 %copy-start.6 = (bf16[128,256]{0,1:T(8,128)(2,1)}, bf16[128,256]{0,1:T(8,128)(2,1)S(1)}, u32[]{:S(2)}) copy-start(bf16[128,256]{0,1:T(8,128)(2,1)S(1)} %constant_dynamic-slice_fusion.18) | copy-start | bytes 196612 | tf_op jit(solution)/shard_map/while
  302.2 5.8 %copy-start.2 = (bf16[128,256]{0,1:T(8,128)(2,1)}, bf16[128,256]{0,1:T(8,128)(2,1)S(1)}, u32[]{:S(2)}) copy-start(bf16[128,256]{0,1:T(8,128)(2,1)S(1)} %copy.55) | copy-start | bytes 196612 | tf_op jit(solution)/shard_map/while
  304.8 8.1 %copy-start.6 = (bf16[128,256]{0,1:T(8,128)(2,1)}, bf16[128,256]{0,1:T(8,128)(2,1)S(1)}, u32[]{:S(2)}) copy-start(bf16[128,256]{0,1:T(8,128)(2,1)S(1)} %constant_dynamic-slice_fusion.18) | copy-start | bytes 196612 | tf_op jit(solution)/shard_map/while
  325.6 5.9 %copy-start.2 = (bf16[128,256]{0,1:T(8,128)(2,1)}, bf16[128,256]{0,1:T(8,128)(2,1)S(1)}, u32[]{:S(2)}) copy-start(bf16[128,256]{0,1:T(8,128)(2,1)S(1)} %copy.55) | copy-start | bytes 196612 | tf_op jit(solution)/shard_map/while
  328.2 8.1 %copy-start.6 = (bf16[128,256]{0,1:T(8,128)(2,1)}, bf16[128,256]{0,1:T(8,128)(2,1)S(1)}, u32[]{:S(2)}) copy-start(bf16[128,256]{0,1:T(8,128)(2,1)S(1)} %constant_dynamic-slice_fusion.18) | copy-start | bytes 196612 | tf_op jit(solution)/shard_map/while
  347.0 19.0 %copy-start.1 = (bf16[2,512,1024]{2,1,0:T(8,128)(2,1)S(1)}, bf16[2,512,1024]{2,1,0:T(8,128)(2,1)}, u32[]{:S(2)}) copy-start(bf16[2,512,1024]{2,1,0:T(8,128)(2,1)} %get-tuple-element.329) | copy-start | bytes 6291460
  348.9 89.1 %copy-start = (bf16[1024,1024]{1,0:T(8,128)(2,1)S(1)}, bf16[1024,1024]{1,0:T(8,128)(2,1)}, u32[]{:S(2)}) copy-start(bf16[1024,1024]{1,0:T(8,128)(2,1)} %all-gather.4.cloned.1.call-done) | copy-start | bytes 6291460
  348.9 89.1 %copy-start.5 = (bf16[128,1024]{0,1:T(8,128)(2,1)S(1)}, bf16[128,1024]{0,1:T(8,128)(2,1)}, u32[]{:S(2)}) copy-start(bf16[128,1024]{0,1:T(8,128)(2,1)} %copy-done.4) | copy-start | bytes 786436
  348.9 28.4 %collective-permute-start.15 = (bf16[2,128,1024]{2,1,0:T(8,128)(2,1)S(1)}, bf16[2,128,1024]{2,1,0:T(8,128)(2,1)S(1)}, u32[]{:S(2)}, u32[]{:S(2)}) collective-permute-start(bf16[2,128,1024]{2,1,0:T(8,128)(2,1)S(1)} %get-tuple-element.488), channel_id=1, source_target_pairs={{0,4},{1,5},{2,6},{3,7},{4,8},{5,9},{6,10},{7,11},{8,12},{9,13},{1... | collective-permute-start | bytes 1572872 | tf_op jit(solution)/shard_map/ppermute | solution.py:26
  354.7 41.1 %collective-permute-start.14 = (bf16[2,128,1024]{2,1,0:T(8,128)(2,1)S(1)}, bf16[2,128,1024]{2,1,0:T(8,128)(2,1)S(1)}, u32[]{:S(2)}, u32[]{:S(2)}) collective-permute-start(bf16[2,128,1024]{2,1,0:T(8,128)(2,1)S(1)} %get-tuple-element.486), channel_id=1, source_target_pairs={{0,3},{1,4},{2,5},{3,6},{4,7},{5,8},{6,9},{7,10},{8,11},{9,12},{10... | collective-permute-start | bytes 1572872 | tf_op jit(solution)/shard_map/ppermute | solution.py:26
  358.3 77.8 %collective-permute-start.13 = (bf16[2,128,1024]{2,1,0:T(8,128)(2,1)S(1)}, bf16[2,128,1024]{2,1,0:T(8,128)(2,1)S(1)}, u32[]{:S(2)}, u32[]{:S(2)}) collective-permute-start(bf16[2,128,1024]{2,1,0:T(8,128)(2,1)S(1)} %get-tuple-element.487), channel_id=1, source_target_pairs={{0,2},{1,3},{2,4},{3,5},{4,6},{5,7},{6,8},{7,9},{8,10},{9,11},{10,... | collective-permute-start | bytes 1572872 | tf_op jit(solution)/shard_map/ppermute | solution.py:26
  361.7 88.2 %collective-permute-start.12 = (bf16[2,128,1024]{2,1,0:T(8,128)(2,1)S(1)}, bf16[2,128,1024]{2,1,0:T(8,128)(2,1)S(1)}, u32[]{:S(2)}, u32[]{:S(2)}) collective-permute-start(bf16[2,128,1024]{2,1,0:T(8,128)(2,1)S(1)} %get-tuple-element.485), channel_id=1, source_target_pairs={{0,1},{1,2},{2,3},{3,4},{4,5},{5,6},{6,7},{7,8},{8,9},{9,10},{10,1... | collective-permute-start | bytes 1572872 | tf_op jit(solution)/shard_map/ppermute | solution.py:26
  366.2 110.5 %copy-start.3 = (f32[2,128,1024]{2,1,0:T(8,128)S(1)}, f32[2,128,1024]{2,1,0:T(8,128)}, u32[]{:S(2)}) copy-start(f32[2,128,1024]{2,1,0:T(8,128)} %get-tuple-element.328) | copy-start | bytes 3145732
  366.2 83.7 %collective-permute-start.11 = (bf16[2,128,1024]{2,1,0:T(8,128)(2,1)S(1)}, bf16[2,128,1024]{2,1,0:T(8,128)(2,1)S(1)}, u32[]{:S(2)}, u32[]{:S(2)}) collective-permute-start(bf16[2,128,1024]{2,1,0:T(8,128)(2,1)S(1)} %get-tuple-element.484), channel_id=1, source_target_pairs={{4,0},{5,1},{6,2},{7,3},{8,4},{9,5},{10,6},{11,7},{12,8},{13,9},{1... | collective-permute-start | bytes 1572872 | tf_op jit(solution)/shard_map/ppermute | solution.py:26
  377.3 72.6 %collective-permute-start.10 = (bf16[2,128,1024]{2,1,0:T(8,128)(2,1)S(1)}, bf16[2,128,1024]{2,1,0:T(8,128)(2,1)S(1)}, u32[]{:S(2)}, u32[]{:S(2)}) collective-permute-start(bf16[2,128,1024]{2,1,0:T(8,128)(2,1)S(1)} %get-tuple-element.482), channel_id=1, source_target_pairs={{3,0},{4,1},{5,2},{6,3},{7,4},{8,5},{9,6},{10,7},{11,8},{12,9},{13... | collective-permute-start | bytes 1572872 | tf_op jit(solution)/shard_map/ppermute | solution.py:26
  395.8 54.1 %collective-permute-start.9 = (bf16[2,128,1024]{2,1,0:T(8,128)(2,1)S(1)}, bf16[2,128,1024]{2,1,0:T(8,128)(2,1)S(1)}, u32[]{:S(2)}, u32[]{:S(2)}) collective-permute-start(bf16[2,128,1024]{2,1,0:T(8,128)(2,1)S(1)} %get-tuple-element.483), channel_id=1, source_target_pairs={{2,0},{3,1},{4,2},{5,3},{6,4},{7,5},{8,6},{9,7},{10,8},{11,9},{12,... | collective-permute-start | bytes 1572872 | tf_op jit(solution)/shard_map/ppermute | solution.py:26
  436.1 40.7 %collective-permute-start.8 = (bf16[2,128,1024]{2,1,0:T(8,128)(2,1)S(1)}, bf16[2,128,1024]{2,1,0:T(8,128)(2,1)S(1)}, u32[]{:S(2)}, u32[]{:S(2)}) collective-permute-start(bf16[2,128,1024]{2,1,0:T(8,128)(2,1)S(1)} %get-tuple-element.481), channel_id=1, source_target_pairs={{1,0},{2,1},{3,2},{4,3},{5,4},{6,5},{7,6},{8,7},{9,8},{10,9},{11,1... | collective-permute-start | bytes 1572872 | tf_op jit(solution)/shard_map/ppermute | solution.py:26
  (30 other events, 85.7 us)
Sparse Core Ops, SparseCore 0:
  31.2 70.5 all-gather.3
  137.1 110.8 reduce-scatter.1
  250.3 258.3 all-gather.5
